TPU v7x, 32 devices: a whole 2x2x4 slice. The times are simulated.
32 devices in a mesh: dp: 4 (over z), row: 2 (over x), col: 4 (over y, core).
Axes of the slice: x: 2, y: 2, z: 4, core: 2. Of those that a mesh axis runs over, the one named last changes fastest.
Arguments:
- tokens: bfloat16 [768, 16384], P('row', ('dp', 'col')), may hold values from -6 to 6
- ln_gain: float32 [768], P('row'), may hold values from 0.5 to 1.5
- ln_bias: float32 [768], P('row'), may hold values from -0.3 to 0.3
- qkv_weight: bfloat16 [768, 3, 768], P('row', None, 'col'), may hold values from -0.21875 to 0.21875
- out_weight: bfloat16 [768, 768], P('col', 'row'), may hold values from -6 to 6
- up_weight: bfloat16 [768, 3072], P('row', 'col'), may hold values from -0.21875 to 0.21875
- down_weight: bfloat16 [768, 3072], P('row', 'col'), may hold values from -0.21875 to 0.21875
- mod_weight: bfloat16 [3, 768, 768], P(None, 'row'), may hold values from -0.109375 to 0.109375
- timestep: int32 [8], replicated, may hold values from 0 to 999
- block_size: int32 [8], replicated, may hold values from 32 to 256, as said below
- cotangent: bfloat16 [768, 16384], P('row', ('dp', 'col')), may hold values from -6 to 6
Outputs:
- output: bfloat16 [768, 16384], P('row', ('dp', 'col'))
- tokens_grad: float32 [768, 16384], P('row', ('dp', 'col'))
- ln_gain_grad: float32 [768], P('row')
- ln_bias_grad: float32 [768], P('row')
- qkv_grad: float32 [768, 3, 768], P('row', None, 'col')
- out_grad: float32 [768, 768], P('col', 'row')
- up_grad: float32 [768, 3072], P('row', 'col')
- down_grad: float32 [768, 3072], P('row', 'col')
- mod_grad: float32 [3, 768, 768], P(None, 'row')
Inputs may be any that keep to these rules, and one draw needn't show every extreme that they name: `block_size`: each entry is 256 halved zero to three times; some sequence has 256.
All inputs are finite; a program needn't handle non-finite values.
Results may differ from a plain program's by a relative error of at most 0.02.
Values may be sent and summed in bfloat16 or wider, within the bound.
No kernel may reach another device: no remote copies, remote signals or barrier semaphores. Data moves between devices by JAX's collectives and lax.ppermute only.
A program may use at most 256 MiB of HBM per device.

v0:
```python
from functools import partial
import math
import jax
import jax.numpy as jnp
from jax import lax
from jax.sharding import PartitionSpec as P

HEAD_DIM = 64
LENGTH = 2048
EPSILON = 1e-05
HIGH = lax.Precision.HIGHEST


def time_embed(steps_in, width_all):
    half_width = width_all // 2
    frequency = jnp.exp(-math.log(10000.0) * jnp.arange(half_width, dtype=jnp.float32) / half_width)
    angles = steps_in.astype(jnp.float32)[:, None] * frequency[None, :]
    return jnp.concatenate([jnp.sin(angles), jnp.cos(angles)], axis=1)


def rope_tables(length, head_width):
    half_dim = head_width // 2
    frequency = jnp.exp(-math.log(10000.0) * jnp.arange(half_dim, dtype=jnp.float32) / half_dim)
    angles = jnp.arange(length, dtype=jnp.float32)[:, None] * frequency[None, :]
    return (jnp.cos(angles), jnp.sin(angles))


def rotate(vector, cosine, sine_tab):
    half_dim = vector.shape[-1] // 2
    front_half, back_half = (vector[..., :half_dim], vector[..., half_dim:])
    return jnp.concatenate(
        [front_half * cosine - back_half * sine_tab, back_half * cosine + front_half * sine_tab],
        axis=-1,
    )


def unrotate(grads_in, cosine, sine_tab):
    half_dim = grads_in.shape[-1] // 2
    front_half, back_half = (grads_in[..., :half_dim], grads_in[..., half_dim:])
    return jnp.concatenate(
        [front_half * cosine + back_half * sine_tab, back_half * cosine - front_half * sine_tab],
        axis=-1,
    )


def token_totals(first_terms, second_terms):
    return lax.psum((jnp.sum(first_terms, axis=1), jnp.sum(second_terms, axis=1)), "row")


def norm_forward(values, width_all):
    sum_plain, sum_square = token_totals(values, values * values)
    mean_row = sum_plain / width_all
    inv_std = lax.rsqrt(sum_square / width_all - mean_row * mean_row + EPSILON)
    return ((values - mean_row[:, None]) * inv_std[:, None], inv_std)


def norm_backward(grad_norm, normed, inv_std, width_all):
    sum_plain, sum_cross = token_totals(grad_norm, grad_norm * normed)
    return inv_std[:, None] * (
        grad_norm - sum_plain[:, None] / width_all - normed * (sum_cross[:, None] / width_all)
    )


def gather_col(local_part):
    return lax.all_gather(local_part, "col", axis=0, tiled=True)


def gather_rows(local_part):
    return lax.all_gather(local_part, "row", axis=0, tiled=True)


def row_product(gathered, tile_part):
    return lax.psum_scatter(
        jnp.dot(gathered, tile_part, preferred_element_type=jnp.float32),
        "row",
        scatter_dimension=0,
        tiled=True,
    )


def col_product(gathered, tile_part):
    return lax.psum_scatter(
        jnp.dot(gathered, tile_part, preferred_element_type=jnp.float32),
        "col",
        scatter_dimension=0,
        tiled=True,
    )


def block_index(block_lens, length):
    positions = jnp.arange(length, dtype=jnp.int32)
    return positions[None, :] // block_lens[:, None]


def masked_scores(query_part, key_rows, key_block, query_block, score_scale):
    scores = (
        jnp.einsum("sqhd,skhd->shqk", query_part, key_rows, preferred_element_type=jnp.float32)
        * score_scale
    )
    visible = key_block[:, None, None, :] <= query_block[:, None, :, None]
    return jnp.where(visible, scores, -1e30)


def attend_forward(queries, key_rows, value_rows, block_lens):
    length = queries.shape[1]
    rows_per = min(512, length)
    score_scale = queries.shape[3] ** (-0.5)
    key_block = block_index(block_lens, length)

    def one_block(offset):
        query_part = lax.dynamic_slice_in_dim(queries, offset, rows_per, 1)
        query_block = lax.dynamic_slice_in_dim(key_block, offset, rows_per, 1)
        scores = masked_scores(query_part, key_rows, key_block, query_block, score_scale)
        row_top = jnp.max(scores, axis=-1, keepdims=True)
        raised = jnp.exp(scores - row_top)
        row_total = jnp.sum(raised, axis=-1, keepdims=True)
        weights = (raised / row_total).astype(jnp.bfloat16)
        block_out = jnp.einsum(
            "shqk,skhd->sqhd", weights, value_rows, preferred_element_type=jnp.float32
        )
        return (block_out, row_top[..., 0] + jnp.log(row_total[..., 0]))

    offsets = jnp.arange(0, length, rows_per, dtype=jnp.int32)
    block_outs, log_totals = lax.map(one_block, offsets)
    return (jnp.moveaxis(block_outs, 0, 1).reshape(queries.shape), log_totals)


def attend_backward(queries, key_rows, value_rows, grad_mixed, log_totals, block_lens):
    length = queries.shape[1]
    rows_per = min(512, length)
    score_scale = queries.shape[3] ** (-0.5)
    key_block = block_index(block_lens, length)

    def one_block(running, element):
        grad_keys, grad_values = running
        offset, log_part = element
        query_part = lax.dynamic_slice_in_dim(queries, offset, rows_per, 1)
        grad_part = lax.dynamic_slice_in_dim(grad_mixed, offset, rows_per, 1)
        query_block = lax.dynamic_slice_in_dim(key_block, offset, rows_per, 1)
        scores = masked_scores(query_part, key_rows, key_block, query_block, score_scale)
        weights = jnp.exp(scores - log_part[..., None])
        grad_weights = jnp.einsum(
            "sqhd,skhd->shqk", grad_part, value_rows, preferred_element_type=jnp.float32
        )
        grad_scores = weights * (
            grad_weights - jnp.sum(weights * grad_weights, axis=-1, keepdims=True)
        )
        grad_scores = grad_scores.astype(jnp.bfloat16)
        grad_query = (
            jnp.einsum("shqk,skhd->sqhd", grad_scores, key_rows, preferred_element_type=jnp.float32)
            * score_scale
        )
        grad_keys = (
            grad_keys
            + jnp.einsum(
                "shqk,sqhd->skhd", grad_scores, query_part, preferred_element_type=jnp.float32
            )
            * score_scale
        )
        grad_values = grad_values + jnp.einsum(
            "shqk,sqhd->skhd",
            weights.astype(jnp.bfloat16),
            grad_part,
            preferred_element_type=jnp.float32,
        )
        return ((grad_keys, grad_values), grad_query)

    offsets = jnp.arange(0, length, rows_per, dtype=jnp.int32)
    zero_grads = jnp.zeros(queries.shape, jnp.float32)
    (grad_keys, grad_values), grad_queries = lax.scan(
        one_block, (zero_grads, zero_grads), (offsets, log_totals)
    )
    return (jnp.moveaxis(grad_queries, 0, 1).reshape(queries.shape), grad_keys, grad_values)


def local(
    tokens,
    ln_gain,
    ln_bias,
    qkv_weight,
    out_weight,
    up_weight,
    down_weight,
    mod_weight,
    timestep,
    block_size,
    cotangent,
):
    n_row = lax.axis_size("row")
    n_col = lax.axis_size("col")
    width_all = mod_weight.shape[2]
    feat_local, local_tokens = tokens.shape
    group_tokens = local_tokens * n_col
    seq_here = group_tokens // n_row // LENGTH
    heads_here = qkv_weight.shape[2] // HEAD_DIM
    group_index = lax.axis_index("dp")
    first_token = group_index * group_tokens + lax.axis_index("col") * local_tokens
    seq_count = max(1, local_tokens // LENGTH)
    token_span = local_tokens // seq_count
    steps_here = lax.dynamic_slice_in_dim(timestep, first_token // LENGTH, seq_count, 0)
    embedded = time_embed(steps_here, width_all)
    modulation = jnp.einsum("nd,ked->kne", embedded, mod_weight.astype(jnp.float32), precision=HIGH)

    def per_token(table):
        return jnp.broadcast_to(table[:, None, :], (seq_count, token_span, feat_local)).reshape(
            local_tokens, feat_local
        )

    def per_sequence(values):
        return jnp.sum(values.reshape(seq_count, token_span, feat_local), axis=1)

    scale_tok = per_token(modulation[0])
    shift_tok = per_token(modulation[1])
    gate_tok = per_token(modulation[2])
    resid = tokens.astype(jnp.float32).T
    norm_one, inv_one = norm_forward(resid, width_all)
    act_one = (norm_one * ln_gain + ln_bias).astype(jnp.bfloat16)
    act_one_all = gather_col(act_one)
    qkv_tile = qkv_weight.reshape(feat_local, -1)
    projected = row_product(act_one_all, qkv_tile).reshape(
        seq_here, LENGTH, 3, heads_here, HEAD_DIM
    )
    cosine, sine_tab = rope_tables(LENGTH, HEAD_DIM)
    cosine = cosine[None, :, None, :]
    sine_tab = sine_tab[None, :, None, :]
    queries = rotate(projected[:, :, 0], cosine, sine_tab).astype(jnp.bfloat16)
    key_rows = rotate(projected[:, :, 1], cosine, sine_tab).astype(jnp.bfloat16)
    value_rows = projected[:, :, 2].astype(jnp.bfloat16)
    seq_first = (group_index * n_row + lax.axis_index("row")) * seq_here
    block_lens = lax.dynamic_slice_in_dim(block_size, seq_first, seq_here, 0)
    attended, log_totals = attend_forward(queries, key_rows, value_rows, block_lens)
    attn_mix = attended.reshape(seq_here * LENGTH, heads_here * HEAD_DIM).astype(jnp.bfloat16)
    attn_mix_all = gather_rows(attn_mix)
    branch_one = col_product(attn_mix_all, out_weight)
    hidden_one = resid + branch_one
    norm_two, inv_two = norm_forward(hidden_one, width_all)
    act_two = (norm_two * (1.0 + scale_tok) + shift_tok).astype(jnp.bfloat16)
    act_two_all = gather_col(act_two)
    pre_act = row_product(act_two_all, up_weight)
    gelu_out = jax.nn.gelu(pre_act, approximate=True).astype(jnp.bfloat16)
    gelu_all = gather_rows(gelu_out)
    branch_two = col_product(gelu_all, down_weight.T)
    result = hidden_one + (1.0 + gate_tok) * branch_two
    grad_out = cotangent.astype(jnp.float32).T
    gate_term = grad_out * branch_two
    grad_two = (grad_out * (1.0 + gate_tok)).astype(jnp.bfloat16)
    grad_two_all = gather_col(grad_two)
    grad_gelu = row_product(grad_two_all, down_weight)
    down_grad = jnp.einsum("td,tf->df", grad_two_all, gelu_all, preferred_element_type=jnp.float32)
    _, gelu_pull = jax.vjp(partial(jax.nn.gelu, approximate=True), pre_act)
    grad_pre = gelu_pull(grad_gelu)[0].astype(jnp.bfloat16)
    grad_pre_all = gather_rows(grad_pre)
    grad_act_two = col_product(grad_pre_all, up_weight.T)
    up_grad = jnp.einsum("td,tf->df", act_two_all, grad_pre_all, preferred_element_type=jnp.float32)
    scale_term = grad_act_two * norm_two
    grad_hidden = grad_out + norm_backward(
        grad_act_two * (1.0 + scale_tok), norm_two, inv_two, width_all
    )
    grad_one = grad_hidden.astype(jnp.bfloat16)
    grad_one_all = gather_col(grad_one)
    grad_attn = row_product(grad_one_all, out_weight.T)
    out_grad = jnp.einsum(
        "tc,td->cd", attn_mix_all, grad_one_all, preferred_element_type=jnp.float32
    )
    grad_attn = grad_attn.astype(jnp.bfloat16).reshape(seq_here, LENGTH, heads_here, HEAD_DIM)
    grad_queries, grad_keys, grad_values = attend_backward(
        queries, key_rows, value_rows, grad_attn, log_totals, block_lens
    )
    grad_queries = unrotate(grad_queries, cosine, sine_tab)
    grad_keys = unrotate(grad_keys, cosine, sine_tab)
    grad_projected = jnp.stack([grad_queries, grad_keys, grad_values], axis=2).astype(jnp.bfloat16)
    grad_projected = grad_projected.reshape(seq_here * LENGTH, 3 * heads_here * HEAD_DIM)
    grad_proj_all = gather_rows(grad_projected)
    grad_act_one = col_product(grad_proj_all, qkv_tile.T)
    qkv_grad = jnp.einsum(
        "td,tk->dk", act_one_all, grad_proj_all, preferred_element_type=jnp.float32
    ).reshape(qkv_weight.shape)
    gain_part = jnp.sum(grad_act_one * norm_one, axis=0)
    bias_part = jnp.sum(grad_act_one, axis=0)
    tokens_grad = grad_hidden + norm_backward(grad_act_one * ln_gain, norm_one, inv_one, width_all)
    grad_mod = jnp.stack(
        [per_sequence(scale_term), per_sequence(grad_act_two), per_sequence(gate_term)]
    )
    mod_part = jnp.einsum("nd,kne->ked", embedded, grad_mod, precision=HIGH)
    gain_grad, bias_grad, mod_grad = (
        lax.psum(gain_part.astype(jnp.bfloat16), ("dp", "col")).astype(jnp.float32),
        lax.psum(bias_part.astype(jnp.bfloat16), ("dp", "col")).astype(jnp.float32),
        lax.psum(mod_part.astype(jnp.bfloat16), ("dp", "col")).astype(jnp.float32),
    )
    qkv_grad, out_grad, up_grad, down_grad = (
        lax.psum(qkv_grad.astype(jnp.bfloat16), "dp").astype(jnp.float32),
        lax.psum(out_grad.astype(jnp.bfloat16), "dp").astype(jnp.float32),
        lax.psum(up_grad.astype(jnp.bfloat16), "dp").astype(jnp.float32),
        lax.psum(down_grad.astype(jnp.bfloat16), "dp").astype(jnp.float32),
    )
    return (
        result.astype(jnp.bfloat16).T,
        tokens_grad.T,
        gain_grad,
        bias_grad,
        qkv_grad,
        out_grad,
        up_grad,
        down_grad,
        mod_grad,
    )


def solution(mesh):
    placed = (
        P("row", ("dp", "col")),
        P("row"),
        P("row"),
        P("row", None, "col"),
        P("col", "row"),
        P("row", "col"),
        P("row", "col"),
        P(None, "row", None),
        P(),
        P(),
        P("row", ("dp", "col")),
    )
    return jax.shard_map(
        local,
        mesh=mesh,
        in_specs=placed,
        out_specs=(
            P("row", ("dp", "col")),
            P("row", ("dp", "col")),
            P("row"),
            P("row"),
            P("row", None, "col"),
            P("col", "row"),
            P("row", "col"),
            P("row", "col"),
            P(None, "row", None),
        ),
        check_vma=False,
    )
```

profile of v0, /device:TPU:0, one launch (start us, length us, event | category | flops | bytes accessed | tf_op | source)
XLA Modules:
  0.0 1632.1 jit_solution(8770067134209926731)
XLA Ops:
  17.3 30.4 %all-gather.9.cloned.1.call-done = bf16[4096,384]{1,0:T(8,128)(2,1)} async-done(((bf16[1024,384]{1,0:T(8,128)(2,1)}), bf16[4096,384]{1,0:T(8,128)(2,1)}) %all-gather.9.cloned.1.call-update) | async-done | bytes 3145744 | tf_op jit(solution)/shard_map/all_gather | solution.py:65
  47.7 7.0 fusion.85
  58.9 106.6 %reduce-scatter.9.cloned.1.call-done = f32[2048,576]{0,1:T(8,128)} async-done(((f32[4096,576]{0,1:T(8,128)}), f32[2048,576]{0,1:T(8,128)}) %reduce-scatter.9.cloned.1.call-update) | async-done | bytes 4718608 | tf_op jit(solution)/shard_map/reduce_scatter | solution.py:73
  170.5 98.7 %while.27 = (s32[]{:T(128)}, bf16[4,1,512,3,64]{2,4,3,1,0:T(8,128)(2,1)}, f32[4,1,3,512]{3,2,1,0:T(4,128)S(1)}, s32[1,2048]{1,0:T(1,128)S(1)}, s32[4]{0:T(128)S(...) while((s32[]{:T(128)}, ...), condition=%wide.region_8.10_spmd, body=%wide.region_5.9_spmd.sunk | while | flops 844102144 | bytes 50471144 | solution.py:124
  173.8 7.0 fusion.137
  180.8 6.8 fusion.138
  187.7 6.7 fusion.139
  198.5 7.0 fusion.137
  205.5 6.8 fusion.138
  212.3 6.7 fusion.139
  223.2 7.0 fusion.137
  230.2 6.8 fusion.138
  237.0 6.7 fusion.139
  247.9 7.0 fusion.137
  254.9 6.8 fusion.138
  261.7 6.7 fusion.139
  272.4 27.1 %all-gather.11.cloned.1.call-done = bf16[4096,192]{0,1:T(8,128)(2,1)} async-done(((bf16[2048,192]{0,1:T(8,128)(2,1)}), bf16[4096,192]{0,1:T(8,128)(2,1)}) %all-gather.11.cloned.1.call-update) | async-done | bytes 1572880 | tf_op jit(solution)/shard_map/all_gather | solution.py:69
  311.7 52.2 %reduce-scatter.11.cloned.1.call-done = f32[1024,384]{1,0:T(8,128)} async-done(((f32[4096,384]{1,0:T(8,128)}), f32[1024,384]{1,0:T(8,128)}) %reduce-scatter.11.cloned.1.call-update) | async-done | bytes 1572880 | tf_op jit(solution)/shard_map/reduce_scatter | solution.py:82
  374.6 19.8 %all-gather.17.cloned.1.call-done = bf16[4096,384]{1,0:T(8,128)(2,1)} async-done(((bf16[1024,384]{1,0:T(8,128)(2,1)}), bf16[4096,384]{1,0:T(8,128)(2,1)}) %all-gather.17.cloned.1.call-update) | async-done | bytes 3145744 | tf_op jit(solution)/shard_map/all_gather | solution.py:65
  394.4 10.4 fusion.89
  404.9 20.0 %all-gather.13.cloned.1.call-done = bf16[4096,384]{1,0:T(8,128)(2,1)} async-done(((bf16[1024,384]{1,0:T(8,128)(2,1)}), bf16[4096,384]{1,0:T(8,128)(2,1)}) %all-gather.13.cloned.1.call-update) | async-done | bytes 3145744 | tf_op jit(solution)/shard_map/all_gather | solution.py:65
  425.0 10.5 fusion.87
  436.0 135.8 %reduce-scatter.17.cloned.1.call-done = f32[2048,768]{1,0:T(8,128)} async-done(((f32[4096,768]{1,0:T(8,128)}), f32[2048,768]{1,0:T(8,128)}) %reduce-scatter.17.cloned.1.call-update) | async-done | bytes 6291472 | tf_op jit(solution)/shard_map/reduce_scatter | solution.py:73
  571.8 146.9 %reduce-scatter.13.cloned.1.call-done = f32[2048,768]{1,0:T(8,128)} async-done(((f32[4096,768]{1,0:T(8,128)}), f32[2048,768]{1,0:T(8,128)}) %reduce-scatter.13.cloned.1.call-update) | async-done | bytes 6291472 | tf_op jit(solution)/shard_map/reduce_scatter | solution.py:73
  718.7 9.0 fusion.51
  728.4 79.9 %all-gather.19.cloned.1.call-done = bf16[4096,768]{1,0:T(8,128)(2,1)} async-done(((bf16[2048,768]{1,0:T(8,128)(2,1)}), bf16[4096,768]{1,0:T(8,128)(2,1)}) %all-gather.19.cloned.1.call-update) | async-done | bytes 6291472 | tf_op jit(solution)/shard_map/all_gather | solution.py:69
  808.3 9.4 fusion.90
  817.7 72.3 %all-gather.15.cloned.1.call-done = bf16[4096,768]{1,0:T(8,128)(2,1)} async-done(((bf16[2048,768]{1,0:T(8,128)(2,1)}), bf16[4096,768]{1,0:T(8,128)(2,1)}) %all-gather.15.cloned.1.call-update) | async-done | bytes 6291472 | tf_op jit(solution)/shard_map/all_gather | solution.py:69
  890.0 9.4 fusion.88
  899.5 52.0 %reduce-scatter.19.cloned.1.call-done = f32[1024,384]{1,0:T(8,128)} async-done(((f32[4096,384]{1,0:T(8,128)}), f32[1024,384]{1,0:T(8,128)}) %reduce-scatter.19.cloned.1.call-update) | async-done | bytes 1572880 | tf_op jit(solution)/shard_map/reduce_scatter | solution.py:82
  959.2 53.5 %reduce-scatter.15.cloned.1.call-done = f32[1024,384]{1,0:T(8,128)} async-done(((f32[4096,384]{1,0:T(8,128)}), f32[1024,384]{1,0:T(8,128)}) %reduce-scatter.15.cloned.1.call-update) | async-done | bytes 1572880 | tf_op jit(solution)/shard_map/reduce_scatter | solution.py:82
  1017.0 28.6 %all-gather.21.cloned.1.call-done = bf16[4096,384]{1,0:T(8,128)(2,1)} async-done(((bf16[1024,384]{1,0:T(8,128)(2,1)}), bf16[4096,384]{1,0:T(8,128)(2,1)}) %all-gather.21.cloned.1.call-update) | async-done | bytes 3145744 | tf_op jit(solution)/shard_map/all_gather | solution.py:65
  1050.5 43.5 %reduce-scatter.21.cloned.1.call-done = f32[2048,192]{0,1:T(8,128)} async-done(((f32[4096,192]{0,1:T(8,128)}), f32[2048,192]{0,1:T(8,128)}) %reduce-scatter.21.cloned.1.call-update) | async-done | bytes 1572880 | tf_op jit(solution)/shard_map/reduce_scatter | solution.py:73
  1096.4 173.6 %while.28 = (s32[]{:T(128)}, f32[1,2048,3,64]{1,3,2,0:T(8,128)}, f32[1,2048,3,64]{1,3,2,0:T(8,128)}, f32[4,1,512,3,64]{2,0,4,3,1:T(4,128)}, s32[4]{0:T(128)S(1)}...) while((s32[]{:T(128)}, f32[1,2048,3,64]{1,3,2,0:T(8,128)}, ...), condition=%wide.region_25.27_spmd.clone, body=%wide.region_23.26_spmd.clone.sunk | while | flops 2063563264 | bytes 151970208 | solution.py:170
  1130.4 8.6 dynamic_update_slice.19
  1145.7 6.3 fusion.150
  1174.1 8.6 dynamic_update_slice.19
  1217.7 8.6 dynamic_update_slice.19
  1261.2 8.6 dynamic_update_slice.19
  1278.4 6.4 convolution_convert_fusion.1
  1284.8 7.1 convolution_convert_fusion
  1297.5 42.6 %all-gather.23.cloned.1.call-done = bf16[4096,576]{0,1:T(8,128)(2,1)} async-done(((bf16[2048,576]{0,1:T(8,128)(2,1)}), bf16[4096,576]{0,1:T(8,128)(2,1)}) %all-gather.23.cloned.1.call-update) | async-done | bytes 4718608 | tf_op jit(solution)/shard_map/all_gather | solution.py:69
  1340.1 6.7 convolution_convert_fusion.2
  1347.1 8.4 fusion.92
  1357.9 82.4 %all-reduce.9.cloned.1.call-done = bf16[3,384,768]{2,1,0:T(8,128)(2,1)} async-done(((bf16[3,384,768]{2,1,0:T(8,128)(2,1)}), bf16[3,384,768]{2,1,0:T(8,128)(2,1)}) %all-reduce.9.cloned.1.call-update) | async-done | bytes 1769488 | tf_op jit(solution)/shard_map/psum | solution.py:288
  1443.8 73.8 %all-reduce.11.cloned.1.call-done = (bf16[384,3,192]{0,2,1:T(8,128)(2,1)}, bf16[192,384]{1,0:T(8,128)(2,1)}, bf16[384,768]{1,0:T(8,128)(2,1)}, bf16[384,768]{1,0:T(8,128)(2,1)}) async-done(((bf16[384,3,192]{0,2,1:T(8,128)(2,1)}, bf16[192,384]{1,0:T(8,128)(2,1)}, bf16[384,768]{1,0:T(8,128)(2,1)}, bf16[384,768]{1,0:T(8,128)(2,1)}), (bf16[384,3,192]{0,2,1:T(8,128)(2,1)}, bf16[192,384]{1,0:T(8,128)(2,1)}, ...) | async-done | bytes 1769488 | tf_op jit(solution)/shard_map/psum | solution.py:291
  1524.6 53.3 %reduce-scatter.23.cloned.1.call-done = f32[1024,384]{1,0:T(8,128)} async-done(((f32[4096,384]{1,0:T(8,128)}), f32[1024,384]{1,0:T(8,128)}) %reduce-scatter.23.cloned.1.call-update) | async-done | bytes 1572880 | tf_op jit(solution)/shard_map/reduce_scatter | solution.py:82
  1580.2 32.1 %all-reduce.4 = (bf16[384]{0:T(512)(128)(2,1)S(1)}, bf16[384]{0:T(512)(128)(2,1)S(1)}) all-reduce(bf16[384]{0:T(512)(128)(2,1)S(1)} %get-tuple-element.173, bf16[384]{0:T(512)(128)(2,1)S(1)} %get-tuple-element.178), channel_id=1, replica_groups=mesh['dp'=4,'row'=2,'col'=4] {'dp','col'}, use_global_device_ids=true, to_apply=%region_32.34 | all-reduce | flops 768 | bytes 3072 | tf_op jit(solution)/shard_map/psum | solution.py:286
  (303 shorter events, 239.1 us)
Async XLA Ops:
  7.2 300.2 %copy-start = (bf16[3,384,768]{2,1,0:T(8,128)(2,1)S(1)}, bf16[3,384,768]{2,1,0:T(8,128)(2,1)}, u32[]{:S(2)}) copy-start(bf16[3,384,768]{2,1,0:T(8,128)(2,1)} %param.24) | copy-start | bytes 5308420
  7.2 8.7 copy-start.34
  7.2 8.7 copy-start.43
  7.2 40.5 %copy-start.28 = (bf16[384,3,192]{0,2,1:T(8,128)(2,1)S(1)}, bf16[384,3,192]{0,2,1:T(8,128)(2,1)}, u32[]{:S(2)}) copy-start(bf16[384,3,192]{0,2,1:T(8,128)(2,1)} %param.20) | copy-start | bytes 1327108
  7.2 40.4 %all-gather.9.cloned.1.call-start = ((), (), s32[]{:S(2)}) async-start(), calls=%async_computation.8 | async-start | bytes 3932160 | tf_op jit(solution)/shard_map/all_gather | solution.py:65
  8.9 45.7 %copy-start.9 = (bf16[384,1024]{0,1:T(8,128)(2,1)}, bf16[384,1024]{0,1:T(8,128)(2,1)S(1)}, u32[]{:S(2)}) copy-start(bf16[384,1024]{0,1:T(8,128)(2,1)S(1)} %copy.24) | copy-start | bytes 2359300
  17.2 148.2 %reduce-scatter.9.cloned.1.call-start = ((), (), s32[]{:S(2)}) async-start(), calls=%async_computation.9 | async-start | bytes 14155776 | tf_op jit(solution)/shard_map/reduce_scatter | solution.py:73
  54.7 244.8 %all-gather.11.cloned.1.call-start = ((), (), s32[]{:S(2)}) async-start(), calls=%async_computation.10 | async-start | bytes 2359296 | tf_op jit(solution)/shard_map/all_gather | solution.py:69
  58.9 110.2 %copy-start.18 = (f32[2048,32]{0,1:T(8,128)}, f32[2048,32]{0,1:T(8,128)S(1)}, u32[]{:S(2)}) copy-start(f32[2048,32]{0,1:T(8,128)S(1)} %get-tuple-element.267) | copy-start | bytes 786436
  58.9 110.2 %copy-start.20 = (f32[2048,32]{0,1:T(8,128)}, f32[2048,32]{0,1:T(8,128)S(1)}, u32[]{:S(2)}) copy-start(f32[2048,32]{0,1:T(8,128)S(1)} %get-tuple-element.268) | copy-start | bytes 786436
  269.3 30.2 %copy-start.27 = (bf16[192,384]{1,0:T(8,128)(2,1)S(1)}, bf16[192,384]{1,0:T(8,128)(2,1)}, u32[]{:S(2)}) copy-start(bf16[192,384]{1,0:T(8,128)(2,1)} %param.21) | copy-start | bytes 442372
  272.2 91.8 %reduce-scatter.11.cloned.1.call-start = ((), (), s32[]{:S(2)}) async-start(), calls=%async_computation.11 | async-start | bytes 7864320 | tf_op jit(solution)/shard_map/reduce_scatter | solution.py:82
  304.9 89.5 %all-gather.17.cloned.1.call-start = ((), (), s32[]{:S(2)}) async-start(), calls=%async_computation.16 | async-start | bytes 3932160 | tf_op jit(solution)/shard_map/all_gather | solution.py:65
  308.9 55.0 %copy-start.10 = (bf16[384,1024]{0,1:T(8,128)(2,1)S(1)}, bf16[384,1024]{0,1:T(8,128)(2,1)}, u32[]{:S(2)}) copy-start(bf16[384,1024]{0,1:T(8,128)(2,1)} %copy-done.9) | copy-start | bytes 2359300
  310.5 56.1 %copy-start.16 = (bf16[384,1024]{0,1:T(8,128)(2,1)}, bf16[384,1024]{0,1:T(8,128)(2,1)S(1)}, u32[]{:S(2)}) copy-start(bf16[384,1024]{0,1:T(8,128)(2,1)S(1)} %copy.26) | copy-start | bytes 2359300
  311.6 113.3 %all-gather.13.cloned.1.call-start = ((), (), s32[]{:S(2)}) async-start(), calls=%async_computation.12 | async-start | bytes 3932160 | tf_op jit(solution)/shard_map/all_gather | solution.py:65
  366.6 27.8 %copy-start.24 = (bf16[384,768]{1,0:T(8,128)(2,1)S(1)}, bf16[384,768]{1,0:T(8,128)(2,1)}, u32[]{:S(2)}) copy-start(bf16[384,768]{1,0:T(8,128)(2,1)} %param.23) | copy-start | bytes 1769476
  374.5 197.3 %reduce-scatter.17.cloned.1.call-start = ((), (), s32[]{:S(2)}) async-start(), calls=%async_computation.17 | async-start | bytes 18874368 | tf_op jit(solution)/shard_map/reduce_scatter | solution.py:73
  404.8 20.1 %copy-start.23 = (bf16[384,768]{1,0:T(8,128)(2,1)S(1)}, bf16[384,768]{1,0:T(8,128)(2,1)}, u32[]{:S(2)}) copy-start(bf16[384,768]{1,0:T(8,128)(2,1)} %param.22) | copy-start | bytes 1769476
  404.9 313.9 %reduce-scatter.13.cloned.1.call-start = ((), (), s32[]{:S(2)}) async-start(), calls=%async_computation.13 | async-start | bytes 18874368 | tf_op jit(solution)/shard_map/reduce_scatter | solution.py:73
  435.5 372.7 %all-gather.19.cloned.1.call-start = ((), (), s32[]{:S(2)}) async-start(), calls=%async_computation.18 | async-start | bytes 9437184 | tf_op jit(solution)/shard_map/all_gather | solution.py:69
  727.8 162.3 %all-gather.15.cloned.1.call-start = ((), (), s32[]{:S(2)}) async-start(), calls=%async_computation.14 | async-start | bytes 9437184 | tf_op jit(solution)/shard_map/all_gather | solution.py:69
  728.3 223.1 %reduce-scatter.19.cloned.1.call-start = ((), (), s32[]{:S(2)}) async-start(), calls=%async_computation.19 | async-start | bytes 7864320 | tf_op jit(solution)/shard_map/reduce_scatter | solution.py:82
  817.6 72.4 %copy-start.25 = (bf16[384,768]{1,0:T(8,128)(2,1)S(1)}, bf16[384,768]{1,0:T(8,128)(2,1)}, u32[]{:S(2)}) copy-start(bf16[384,768]{1,0:T(8,128)(2,1)} %param.23) | copy-start | bytes 1769476
  817.7 195.0 %reduce-scatter.15.cloned.1.call-start = ((), (), s32[]{:S(2)}) async-start(), calls=%async_computation.15 | async-start | bytes 7864320 | tf_op jit(solution)/shard_map/reduce_scatter | solution.py:82
  899.4 52.0 %copy-start.12 = (f32[1024,384]{1,0:T(8,128)S(1)}, f32[1024,384]{1,0:T(8,128)}, u32[]{:S(2)}) copy-start(f32[1024,384]{1,0:T(8,128)} %get-tuple-element.238) | copy-start | bytes 4718596
  899.4 146.2 %all-gather.21.cloned.1.call-start = ((), (), s32[]{:S(2)}) async-start(), calls=%async_computation.20 | async-start | bytes 3932160 | tf_op jit(solution)/shard_map/all_gather | solution.py:65
  1016.9 77.1 %reduce-scatter.21.cloned.1.call-start = ((), (), s32[]{:S(2)}) async-start(), calls=%async_computation.21 | async-start | bytes 4718592 | tf_op jit(solution)/shard_map/reduce_scatter | solution.py:73
  1050.4 289.7 %all-gather.23.cloned.1.call-start = ((), (), s32[]{:S(2)}) async-start(), calls=%async_computation.22 | async-start | bytes 7077888 | tf_op jit(solution)/shard_map/all_gather | solution.py:69
  1126.4 12.6 copy-start.5
  1126.4 12.6 copy-start.8
  1169.5 13.2 copy-start.5
  1169.5 13.2 copy-start.8
  1213.1 13.2 copy-start.5
  1213.1 13.2 copy-start.8
  1256.6 13.2 copy-start.5
  1256.6 13.2 copy-start.8
  1277.3 162.9 %all-reduce.9.cloned.1.call-start = ((), (), s32[]{:S(2)}) async-start(), calls=%async_computation.24 | async-start | bytes 3538944 | tf_op jit(solution)/shard_map/psum | solution.py:288
  1284.8 7.1 copy-start.42
  1284.8 7.1 copy-start.41
  1284.8 7.2 copy-start.40
  1293.5 224.1 %all-reduce.11.cloned.1.call-start = ((), (), s32[]{:S(2)}) async-start(), calls=%async_computation.25 | async-start | bytes 3538944 | tf_op jit(solution)/shard_map/psum | solution.py:291
  1297.5 49.7 %copy-start.29 = (bf16[384,3,192]{0,2,1:T(8,128)(2,1)S(1)}, bf16[384,3,192]{0,2,1:T(8,128)(2,1)}, u32[]{:S(2)}) copy-start(bf16[384,3,192]{0,2,1:T(8,128)(2,1)} %param.20) | copy-start | bytes 1327108
  1346.8 231.1 %reduce-scatter.23.cloned.1.call-start = ((), (), s32[]{:S(2)}) async-start(), calls=%async_computation.23 | async-start | bytes 7864320 | tf_op jit(solution)/shard_map/reduce_scatter | solution.py:82
  1443.8 134.1 %copy-start.11 = (bf16[384,1024]{0,1:T(8,128)(2,1)S(1)}, bf16[384,1024]{0,1:T(8,128)(2,1)}, u32[]{:S(2)}) copy-start(bf16[384,1024]{0,1:T(8,128)(2,1)} %copy-done.9) | copy-start | bytes 2359300
  1443.8 134.1 %copy-start.31 = (f32[1024]{0:T(1024)S(1)}, f32[1024]{0:T(1024)}, u32[]{:S(2)}) copy-start(f32[1024]{0:T(1024)} %copy-done.30) | copy-start | bytes 12292
  1443.8 134.1 %copy-start.33 = (f32[1024]{0:T(1024)S(1)}, f32[1024]{0:T(1024)}, u32[]{:S(2)}) copy-start(f32[1024]{0:T(1024)} %copy-done.32) | copy-start | bytes 12292
  1443.8 134.1 %copy-start.35 = (f32[384]{0:T(512)S(1)}, f32[384]{0:T(512)}, u32[]{:S(2)}) copy-start(f32[384]{0:T(512)} %param.18) | copy-start | bytes 4612
  (40 other events, 157.2 us)
Sparse Core Ops, SparseCore 0:
  17.3 30.2 all-gather.8
  54.8 110.6 reduce-scatter.8
  272.3 27.1 all-gather.10
  305.0 58.8 reduce-scatter.10
  365.9 28.4 all-gather.16
  396.4 28.4 all-gather.12
  427.3 144.5 reduce-scatter.16
  574.1 144.5 reduce-scatter.12
  727.9 80.3 all-gather.18
  809.6 80.3 all-gather.14
  892.6 58.8 reduce-scatter.18
  953.8 58.8 reduce-scatter.14
  1017.1 28.5 all-gather.20
  1050.6 43.3 reduce-scatter.20
  1277.4 62.6 all-gather.22
  1343.5 96.7 all-reduce.8
  1443.3 74.3 all-reduce.10
  1520.0 57.8 reduce-scatter.22
where the time goes:
time: 1640 us; the launch traced here: 1630 us
  waiting for transfers between devices  1120 us (68%)
  matrix products  243 us (15%)
  other arithmetic  111 us (7%)
  local copies, waits for them, and re-layouts  68.2 us (4%)
  blocking collectives  53.1 us (3%)
  between operations  16.6 us (1%)
  loops' own time  16.4 us (1%)
    reduce_scatter x4, waiting for transfers between devices, row_product(): lax.psum_scatter(jnp.dot(gathered, tile_part, preferred_element_type=jnp....  433 us
    all_gather x4, waiting for transfers between devices, gather_rows(): return lax.all_gather(local_part, 'row', axis=0, tiled=True)  222 us
    reduce_scatter x4, waiting for transfers between devices, col_product(): lax.psum_scatter(jnp.dot(gathered, tile_part, preferred_element_type=jnp....  211 us
    all_gather x4, waiting for transfers between devices, gather_col(): return lax.all_gather(local_part, 'col', axis=0, tiled=True)  98.9 us
    psum x1, waiting for transfers between devices, local(): lax.psum(mod_part.astype(jnp.bfloat16), ('dp', 'col')).astype(jnp.float32)  82.4 us
    psum x1, waiting for transfers between devices, local(): lax.psum(qkv_grad.astype(jnp.bfloat16), 'dp').astype(jnp.float32)  73.8 us
    dot_general x8, matrix products, masked_scores(): jnp.einsum('sqhd,skhd->shqk', query_part, key_rows, preferred_element_typ...  40.6 us
    dynamic_update_slice x8, local copies, waits for them, and re-layouts, attend_forward(): block_outs, log_totals = lax.map(one_block, offsets)  36.1 us
  transfers between devices with their start and end apart: 18, of which 18 were waited for; matrix products, arithmetic and copies ran while one was open for 6% of the time, Pallas kernels for 0%

commit v1 on v0

--- a/solution.py
+++ b/solution.py
@@ -11,6 +11,35 @@
 HIGH = lax.Precision.HIGHEST
 
 
+def advance_steps_all(u_in, k_dim):
+    u_in = jnp.moveaxis(u_in, 0, k_dim)
+    q_next = u_in.shape
+    piece_out = u_in.reshape(
+        *q_next[:k_dim], q_next[k_dim] * q_next[k_dim + 1], *q_next[k_dim + 2 :]
+    )
+    return piece_out
+
+
+def _fill_trees(x_in, a_name):
+    upper = jax.lax.axis_size(a_name)
+    moved, tall = (upper, jax.lax.axis_index(a_name))
+    all_values, small = (x_in[None], 1)
+    while small < moved:
+        extra = list(map(lambda k0: (k0, k0 ^ small), range(moved)))
+        u_next = jax.lax.ppermute(all_values, a_name, extra)
+        part_now = tall & small == 0
+        all_values = jnp.concatenate(
+            [jnp.where(part_now, all_values, u_next), jnp.where(part_now, u_next, all_values)]
+        )
+        small *= 2
+    return all_values
+
+
+def balance_cards_on(sample, s0, dim_i):
+    x_new = advance_steps_all(_fill_trees(sample, s0), dim_i)
+    return x_new
+
+
 def time_embed(steps_in, width_all):
     half_width = width_all // 2
     frequency = jnp.exp(-math.log(10000.0) * jnp.arange(half_width, dtype=jnp.float32) / half_width)
@@ -66,7 +95,7 @@
 
 
 def gather_rows(local_part):
-    return lax.all_gather(local_part, "row", axis=0, tiled=True)
+    return balance_cards_on(local_part, "row", 0)
 
 
 def row_product(gathered, tile_part):

time: 1640 us -> 1510 us (0.921)
  waiting for transfers between devices: 1120 us -> 991 us
  matrix products: 243 us -> 224 us
    all_gather x4 -> x0, waiting for transfers between devices: 222 us -> none  [gather_rows(): return lax.all_gather(local_part, 'row', axis=0, tiled=True)]
    ppermute x0 -> x4, waiting for transfers between devices: none -> 196 us  [_fill_trees(): u_next = jax.lax.ppermute(all_values, a_name, extra)]
    reduce_scatter x4, waiting for transfers between devices: 211 us -> 155 us  [col_product(): lax.psum_scatter(jnp.dot(gathered, tile_part, preferred_element_type=jnp....]
    psum x1, waiting for transfers between devices: 82.4 us -> 33.5 us  [local(): lax.psum(mod_part.astype(jnp.bfloat16), ('dp', 'col')).astype(jnp.float32)]
  transfers between devices with their start and end apart: 18 -> 18, of which waited for: 18 -> 17; matrix products, arithmetic and copies ran while one was open for 6% -> 6% of each run, Pallas kernels for 0% -> 0%
where the time goes in v1:
time: 1510 us; the launch traced here: 1500 us
  waiting for transfers between devices  991 us (66%)
  matrix products  224 us (15%)
  other arithmetic  120 us (8%)
  local copies, waits for them, and re-layouts  80.8 us (5%)
  blocking collectives  53.1 us (4%)
  loops' own time  16.4 us (1%)
  between operations  16.2 us (1%)
    reduce_scatter x4, waiting for transfers between devices, row_product(): lax.psum_scatter(jnp.dot(gathered, tile_part, preferred_element_type=jnp....  433 us
    ppermute x4, waiting for transfers between devices, _fill_trees(): u_next = jax.lax.ppermute(all_values, a_name, extra)  196 us
    reduce_scatter x4, waiting for transfers between devices, col_product(): lax.psum_scatter(jnp.dot(gathered, tile_part, preferred_element_type=jnp....  155 us
    all_gather x4, waiting for transfers between devices, gather_col(): return lax.all_gather(local_part, 'col', axis=0, tiled=True)  98.9 us
    psum x1, waiting for transfers between devices, local(): lax.psum(qkv_grad.astype(jnp.bfloat16), 'dp').astype(jnp.float32)  74 us
    dot_general x8, matrix products, masked_scores(): jnp.einsum('sqhd,skhd->shqk', query_part, key_rows, preferred_element_typ...  40.3 us
    dynamic_update_slice x8, local copies, waits for them, and re-layouts, attend_forward(): block_outs, log_totals = lax.map(one_block, offsets)  36.1 us
    psum x1, waiting for transfers between devices, local(): lax.psum(mod_part.astype(jnp.bfloat16), ('dp', 'col')).astype(jnp.float32)  33.5 us
  transfers between devices with their start and end apart: 18, of which 17 were waited for; matrix products, arithmetic and copies ran while one was open for 6% of the time, Pallas kernels for 0%

profile of v1, /device:TPU:0, one launch (start us, length us, event | category | flops | bytes accessed | tf_op | source)
XLA Modules:
  0.0 1504.6 jit_solution(12911043304762869255)
XLA Ops:
  17.3 30.4 %all-gather.5.cloned.1.call-done = bf16[4096,384]{1,0:T(8,128)(2,1)} async-done(((bf16[1024,384]{1,0:T(8,128)(2,1)}), bf16[4096,384]{1,0:T(8,128)(2,1)}) %all-gather.5.cloned.1.call-update) | async-done | bytes 3145744 | tf_op jit(solution)/shard_map/all_gather | solution.py:94
  47.7 7.0 fusion.92
  58.9 106.6 %reduce-scatter.9.cloned.1.call-done = f32[2048,576]{0,1:T(8,128)} async-done(((f32[4096,576]{0,1:T(8,128)}), f32[2048,576]{0,1:T(8,128)}) %reduce-scatter.9.cloned.1.call-update) | async-done | bytes 4718608 | tf_op jit(solution)/shard_map/reduce_scatter | solution.py:102
  170.6 98.4 %while.27 = (s32[]{:T(128)}, bf16[4,1,512,3,64]{2,4,3,1,0:T(8,128)(2,1)}, f32[4,1,3,512]{3,2,1,0:T(4,128)S(1)}, s32[1,2048]{1,0:T(1,128)S(1)}, s32[4]{0:T(128)S(...) while((s32[]{:T(128)}, ...), condition=%wide.region_8.10_spmd, body=%wide.region_5.9_spmd.sunk | while | flops 844102144 | bytes 50471144 | solution.py:153
  173.8 6.9 fusion.143
  180.7 6.8 fusion.144
  187.6 6.7 fusion.145
  198.4 6.9 fusion.143
  205.3 6.8 fusion.144
  212.2 6.7 fusion.145
  223.0 6.9 fusion.143
  230.0 6.8 fusion.144
  236.8 6.7 fusion.145
  247.6 6.9 fusion.143
  254.5 6.8 fusion.144
  261.4 6.7 fusion.145
  274.7 19.1 %collective-permute-done = bf16[1,2048,192]{1,2,0:T(8,128)(2,1)} collective-permute-done((bf16[1,2048,192]{1,2,0:T(8,128)(2,1)}, bf16[1,2048,192]{1,2,0:T(8,128)(2,1)}, u32[]{:S(2)}, u32[]{:S(2)}) %collective-permute-start) | collective-permute-done | bytes 786464 | tf_op jit(solution)/shard_map/ppermute | solution.py:29
  307.6 52.2 %reduce-scatter.11.cloned.1.call-done = f32[1024,384]{1,0:T(8,128)} async-done(((f32[4096,384]{1,0:T(8,128)}), f32[1024,384]{1,0:T(8,128)}) %reduce-scatter.11.cloned.1.call-update) | async-done | bytes 1572880 | tf_op jit(solution)/shard_map/reduce_scatter | solution.py:111
  370.4 19.9 %all-gather.9.cloned.1.call-done = bf16[4096,384]{1,0:T(8,128)(2,1)} async-done(((bf16[1024,384]{1,0:T(8,128)(2,1)}), bf16[4096,384]{1,0:T(8,128)(2,1)}) %all-gather.9.cloned.1.call-update) | async-done | bytes 3145744 | tf_op jit(solution)/shard_map/all_gather | solution.py:94
  390.3 10.4 fusion.96
  400.8 20.0 %all-gather.7.cloned.1.call-done = bf16[4096,384]{1,0:T(8,128)(2,1)} async-done(((bf16[1024,384]{1,0:T(8,128)(2,1)}), bf16[4096,384]{1,0:T(8,128)(2,1)}) %all-gather.7.cloned.1.call-update) | async-done | bytes 3145744 | tf_op jit(solution)/shard_map/all_gather | solution.py:94
  420.8 10.5 fusion.94
  431.8 135.7 %reduce-scatter.17.cloned.1.call-done = f32[2048,768]{1,0:T(8,128)} async-done(((f32[4096,768]{1,0:T(8,128)}), f32[2048,768]{1,0:T(8,128)}) %reduce-scatter.17.cloned.1.call-update) | async-done | bytes 6291472 | tf_op jit(solution)/shard_map/reduce_scatter | solution.py:102
  567.6 146.9 %reduce-scatter.13.cloned.1.call-done = f32[2048,768]{1,0:T(8,128)} async-done(((f32[4096,768]{1,0:T(8,128)}), f32[2048,768]{1,0:T(8,128)}) %reduce-scatter.13.cloned.1.call-update) | async-done | bytes 6291472 | tf_op jit(solution)/shard_map/reduce_scatter | solution.py:102
  714.4 8.5 fusion.55
  723.3 69.3 %collective-permute-done.2 = bf16[1,2048,768]{2,1,0:T(8,128)(2,1)S(1)} collective-permute-done((bf16[1,2048,768]{2,1,0:T(8,128)(2,1)S(1)}, bf16[1,2048,768]{2,1,0:T(8,128)(2,1)S(1)}, u32[]{:S(2)}, u32[]{:S(2)}) %collective-permute-start.2) | collective-permute-done | bytes 3145760 | tf_op jit(solution)/shard_map/ppermute | solution.py:29
  802.3 68.5 %collective-permute-done.1 = bf16[1,2048,768]{2,1,0:T(8,128)(2,1)S(1)} collective-permute-done((bf16[1,2048,768]{2,1,0:T(8,128)(2,1)}, bf16[1,2048,768]{2,1,0:T(8,128)(2,1)S(1)}, u32[]{:S(2)}, u32[]{:S(2)}) %collective-permute-start.1) | collective-permute-done | bytes 3145760 | tf_op jit(solution)/shard_map/ppermute | solution.py:29
  890.9 49.9 %reduce-scatter.15.cloned.1.call-done = f32[1024,384]{1,0:T(8,128)} async-done(((f32[4096,384]{1,0:T(8,128)}), f32[1024,384]{1,0:T(8,128)}) %reduce-scatter.15.cloned.1.call-update) | async-done | bytes 1572880 | tf_op jit(solution)/shard_map/reduce_scatter | solution.py:111
  945.2 28.6 %all-gather.11.cloned.1.call-done = bf16[4096,384]{1,0:T(8,128)(2,1)} async-done(((bf16[1024,384]{1,0:T(8,128)(2,1)}), bf16[4096,384]{1,0:T(8,128)(2,1)}) %all-gather.11.cloned.1.call-update) | async-done | bytes 3145744 | tf_op jit(solution)/shard_map/all_gather | solution.py:94
  978.7 43.5 %reduce-scatter.21.cloned.1.call-done = f32[2048,192]{0,1:T(8,128)} async-done(((f32[4096,192]{0,1:T(8,128)}), f32[2048,192]{0,1:T(8,128)}) %reduce-scatter.21.cloned.1.call-update) | async-done | bytes 1572880 | tf_op jit(solution)/shard_map/reduce_scatter | solution.py:102
  1024.6 173.9 %while.28 = (s32[]{:T(128)}, f32[1,2048,3,64]{1,3,2,0:T(8,128)}, f32[1,2048,3,64]{1,3,2,0:T(8,128)}, f32[4,1,512,3,64]{2,0,4,3,1:T(4,128)}, s32[4]{0:T(128)S(1)}...) while((s32[]{:T(128)}, f32[1,2048,3,64]{1,3,2,0:T(8,128)}, ...), condition=%wide.region_25.27_spmd.clone, body=%wide.region_23.26_spmd.clone.sunk | while | flops 2063563264 | bytes 151970208 | solution.py:199
  1043.3 6.2 multiply_convert_fusion.4
  1058.7 8.6 dynamic_update_slice.19
  1073.9 6.4 fusion.156
  1086.4 6.2 multiply_convert_fusion.4
  1102.4 8.6 dynamic_update_slice.19
  1117.6 6.4 fusion.156
  1130.2 6.2 multiply_convert_fusion.4
  1146.1 8.6 dynamic_update_slice.19
  1161.3 6.4 fusion.156
  1173.8 6.2 multiply_convert_fusion.4
  1189.7 8.6 dynamic_update_slice.19
  1219.9 39.2 %collective-permute-done.3 = bf16[1,2048,576]{1,2,0:T(8,128)(2,1)} collective-permute-done((bf16[1,2048,576]{1,2,0:T(8,128)(2,1)}, bf16[1,2048,576]{1,2,0:T(8,128)(2,1)}, u32[]{:S(2)}, u32[]{:S(2)}) %collective-permute-start.3) | collective-permute-done | bytes 2359328 | tf_op jit(solution)/shard_map/ppermute | solution.py:29
  1269.0 8.3 fusion.99
  1279.5 33.5 %all-reduce.9.cloned.1.call-done = bf16[3,384,768]{2,1,0:T(8,128)(2,1)} async-done(((bf16[3,384,768]{2,1,0:T(8,128)(2,1)}), bf16[3,384,768]{2,1,0:T(8,128)(2,1)}) %all-reduce.9.cloned.1.call-update) | async-done | bytes 1769488 | tf_op jit(solution)/shard_map/psum | solution.py:317
  1316.7 74.0 %all-reduce.11.cloned.1.call-done = (bf16[384,3,192]{0,2,1:T(8,128)(2,1)}, bf16[192,384]{1,0:T(8,128)(2,1)}, bf16[384,768]{1,0:T(8,128)(2,1)}, bf16[384,768]{1,0:T(8,128)(2,1)}) async-done(((bf16[384,3,192]{0,2,1:T(8,128)(2,1)}, bf16[192,384]{1,0:T(8,128)(2,1)}, bf16[384,768]{1,0:T(8,128)(2,1)}, bf16[384,768]{1,0:T(8,128)(2,1)}), (bf16[384,3,192]{0,2,1:T(8,128)(2,1)}, bf16[192,384]{1,0:T(8,128)(2,1)}, ...) | async-done | bytes 1769488 | tf_op jit(solution)/shard_map/psum | solution.py:320
  1397.6 53.3 %reduce-scatter.23.cloned.1.call-done = f32[1024,384]{1,0:T(8,128)} async-done(((f32[4096,384]{1,0:T(8,128)}), f32[1024,384]{1,0:T(8,128)}) %reduce-scatter.23.cloned.1.call-update) | async-done | bytes 1572880 | tf_op jit(solution)/shard_map/reduce_scatter | solution.py:111
  1453.2 32.1 %all-reduce.4 = (bf16[384]{0:T(512)(128)(2,1)S(1)}, bf16[384]{0:T(512)(128)(2,1)S(1)}) all-reduce(bf16[384]{0:T(512)(128)(2,1)S(1)} %get-tuple-element.182, bf16[384]{0:T(512)(128)(2,1)S(1)} %get-tuple-element.187), channel_id=1, replica_groups=mesh['dp'=4,'row'=2,'col'=4] {'dp','col'}, use_global_device_ids=true, to_apply=%region_32.34 | all-reduce | flops 768 | bytes 3072 | tf_op jit(solution)/shard_map/psum | solution.py:315
  (329 shorter events, 244.5 us)
Async XLA Ops:
  7.2 296.1 %copy-start = (bf16[3,384,768]{2,1,0:T(8,128)(2,1)S(1)}, bf16[3,384,768]{2,1,0:T(8,128)(2,1)}, u32[]{:S(2)}) copy-start(bf16[3,384,768]{2,1,0:T(8,128)(2,1)} %param.24) | copy-start | bytes 5308420
  7.2 8.7 copy-start.39
  7.2 8.7 copy-start.48
  7.2 40.5 %copy-start.33 = (bf16[384,3,192]{0,2,1:T(8,128)(2,1)S(1)}, bf16[384,3,192]{0,2,1:T(8,128)(2,1)}, u32[]{:S(2)}) copy-start(bf16[384,3,192]{0,2,1:T(8,128)(2,1)} %param.20) | copy-start | bytes 1327108
  7.2 40.4 %all-gather.5.cloned.1.call-start = ((), (), s32[]{:S(2)}) async-start(), calls=%async_computation.8 | async-start | bytes 3932160 | tf_op jit(solution)/shard_map/all_gather | solution.py:94
  8.9 45.7 %copy-start.11 = (bf16[384,1024]{0,1:T(8,128)(2,1)}, bf16[384,1024]{0,1:T(8,128)(2,1)S(1)}, u32[]{:S(2)}) copy-start(bf16[384,1024]{0,1:T(8,128)(2,1)S(1)} %copy.32) | copy-start | bytes 2359300
  17.2 148.3 %reduce-scatter.9.cloned.1.call-start = ((), (), s32[]{:S(2)}) async-start(), calls=%async_computation.9 | async-start | bytes 14155776 | tf_op jit(solution)/shard_map/reduce_scatter | solution.py:102
  54.7 305.1 %reduce-scatter.11.cloned.1.call-start = ((), (), s32[]{:S(2)}) async-start(), calls=%async_computation.10 | async-start | bytes 7864320 | tf_op jit(solution)/shard_map/reduce_scatter | solution.py:111
  58.9 110.2 %copy-start.23 = (f32[2048,32]{0,1:T(8,128)}, f32[2048,32]{0,1:T(8,128)S(1)}, u32[]{:S(2)}) copy-start(f32[2048,32]{0,1:T(8,128)S(1)} %get-tuple-element.284) | copy-start | bytes 786436
  58.9 110.2 %copy-start.25 = (f32[2048,32]{0,1:T(8,128)}, f32[2048,32]{0,1:T(8,128)S(1)}, u32[]{:S(2)}) copy-start(f32[2048,32]{0,1:T(8,128)S(1)} %get-tuple-element.285) | copy-start | bytes 786436
  180.7 6.8 copy-start.26
  205.3 6.8 copy-start.26
  229.9 6.8 copy-start.26
  254.5 6.8 copy-start.26
  274.4 19.4 %collective-permute-start = (bf16[1,2048,192]{1,2,0:T(8,128)(2,1)}, bf16[1,2048,192]{1,2,0:T(8,128)(2,1)}, u32[]{:S(2)}, u32[]{:S(2)}) collective-permute-start(bf16[1,2048,192]{1,2,0:T(8,128)(2,1)} %convert_element_type.146), channel_id=1, source_target_pairs={{0,4},{4,0},{1,5},{5,1},{2,6},{6,2},{3,7},{7,3},{8,12},{12,8},{9,1... | collective-permute-start | bytes 2359304 | tf_op jit(solution)/shard_map/ppermute | solution.py:29
  300.7 89.6 %all-gather.9.cloned.1.call-start = ((), (), s32[]{:S(2)}) async-start(), calls=%async_computation.14 | async-start | bytes 3932160 | tf_op jit(solution)/shard_map/all_gather | solution.py:94
  304.8 55.0 %copy-start.12 = (bf16[384,1024]{0,1:T(8,128)(2,1)S(1)}, bf16[384,1024]{0,1:T(8,128)(2,1)}, u32[]{:S(2)}) copy-start(bf16[384,1024]{0,1:T(8,128)(2,1)} %copy-done.11) | copy-start | bytes 2359300
  306.4 56.1 %copy-start.19 = (bf16[384,1024]{0,1:T(8,128)(2,1)}, bf16[384,1024]{0,1:T(8,128)(2,1)S(1)}, u32[]{:S(2)}) copy-start(bf16[384,1024]{0,1:T(8,128)(2,1)S(1)} %copy.35) | copy-start | bytes 2359300
  307.5 113.3 %all-gather.7.cloned.1.call-start = ((), (), s32[]{:S(2)}) async-start(), calls=%async_computation.11 | async-start | bytes 3932160 | tf_op jit(solution)/shard_map/all_gather | solution.py:94
  362.5 27.8 %copy-start.29 = (bf16[384,768]{1,0:T(8,128)(2,1)S(1)}, bf16[384,768]{1,0:T(8,128)(2,1)}, u32[]{:S(2)}) copy-start(bf16[384,768]{1,0:T(8,128)(2,1)} %param.23) | copy-start | bytes 1769476
  370.4 197.2 %reduce-scatter.17.cloned.1.call-start = ((), (), s32[]{:S(2)}) async-start(), calls=%async_computation.15 | async-start | bytes 18874368 | tf_op jit(solution)/shard_map/reduce_scatter | solution.py:102
  400.7 20.1 %copy-start.28 = (bf16[384,768]{1,0:T(8,128)(2,1)S(1)}, bf16[384,768]{1,0:T(8,128)(2,1)}, u32[]{:S(2)}) copy-start(bf16[384,768]{1,0:T(8,128)(2,1)} %param.22) | copy-start | bytes 1769476
  400.8 313.7 %reduce-scatter.13.cloned.1.call-start = ((), (), s32[]{:S(2)}) async-start(), calls=%async_computation.12 | async-start | bytes 18874368 | tf_op jit(solution)/shard_map/reduce_scatter | solution.py:102
  431.4 450.5 %reduce-scatter.19.cloned.1.call-start = ((), (), s32[]{:S(2)}) async-start(), calls=%async_computation.16 | async-start | bytes 7864320 | tf_op jit(solution)/shard_map/reduce_scatter | solution.py:111
  722.9 69.7 %collective-permute-start.2 = (bf16[1,2048,768]{2,1,0:T(8,128)(2,1)S(1)}, bf16[1,2048,768]{2,1,0:T(8,128)(2,1)S(1)}, u32[]{:S(2)}, u32[]{:S(2)}) collective-permute-start(bf16[1,2048,768]{2,1,0:T(8,128)(2,1)S(1)} %get-tuple-element.254), channel_id=1, source_target_pairs={{0,4},{4,0},{1,5},{5,1},{2,6},{6,2},{3,7},{7,3},{8,12},{12,8},{9,1... | collective-permute-start | bytes 9437192 | tf_op jit(solution)/shard_map/ppermute | solution.py:29
  801.7 139.2 %reduce-scatter.15.cloned.1.call-start = ((), (), s32[]{:S(2)}) async-start(), calls=%async_computation.13 | async-start | bytes 7864320 | tf_op jit(solution)/shard_map/reduce_scatter | solution.py:111
  801.7 69.1 %collective-permute-start.1 = (bf16[1,2048,768]{2,1,0:T(8,128)(2,1)}, bf16[1,2048,768]{2,1,0:T(8,128)(2,1)S(1)}, u32[]{:S(2)}, u32[]{:S(2)}) collective-permute-start(bf16[1,2048,768]{2,1,0:T(8,128)(2,1)} %get-tuple-element.255), channel_id=1, source_target_pairs={{0,4},{4,0},{1,5},{5,1},{2,6},{6,2},{3,7},{7,3},{8,12},{12,8},{9,1... | collective-permute-start | bytes 9437192 | tf_op jit(solution)/shard_map/ppermute | solution.py:29
  881.8 91.9 %all-gather.11.cloned.1.call-start = ((), (), s32[]{:S(2)}) async-start(), calls=%async_computation.17 | async-start | bytes 3932160 | tf_op jit(solution)/shard_map/all_gather | solution.py:94
  945.1 77.0 %reduce-scatter.21.cloned.1.call-start = ((), (), s32[]{:S(2)}) async-start(), calls=%async_computation.18 | async-start | bytes 4718592 | tf_op jit(solution)/shard_map/reduce_scatter | solution.py:102
  978.6 334.5 %all-reduce.9.cloned.1.call-start = ((), (), s32[]{:S(2)}) async-start(), calls=%async_computation.20 | async-start | bytes 3538944 | tf_op jit(solution)/shard_map/psum | solution.py:317
  1024.7 6.6 copy-start.4
  1024.7 6.6 copy-start.9
  1054.6 12.6 copy-start.5
  1054.6 12.6 copy-start.10
  1097.8 13.2 copy-start.5
  1097.8 13.2 copy-start.10
  1141.5 13.2 copy-start.5
  1141.5 13.2 copy-start.10
  1185.1 13.2 copy-start.5
  1185.1 13.2 copy-start.10
  1204.3 6.8 slice-start.2
  1206.0 53.1 %collective-permute-start.3 = (bf16[1,2048,576]{1,2,0:T(8,128)(2,1)}, bf16[1,2048,576]{1,2,0:T(8,128)(2,1)}, u32[]{:S(2)}, u32[]{:S(2)}) collective-permute-start(bf16[1,2048,576]{1,2,0:T(8,128)(2,1)} %bitcast.32), channel_id=1, source_target_pairs={{0,4},{4,0},{1,5},{5,1},{2,6},{6,2},{3,7},{7,3},{8,12},{12,8},{9,1... | collective-permute-start | bytes 7077896 | tf_op jit(solution)/shard_map/ppermute | solution.py:29
  1216.2 174.4 %all-reduce.11.cloned.1.call-start = ((), (), s32[]{:S(2)}) async-start(), calls=%async_computation.21 | async-start | bytes 3538944 | tf_op jit(solution)/shard_map/psum | solution.py:320
  1268.6 182.2 %reduce-scatter.23.cloned.1.call-start = ((), (), s32[]{:S(2)}) async-start(), calls=%async_computation.19 | async-start | bytes 7864320 | tf_op jit(solution)/shard_map/reduce_scatter | solution.py:111
  1316.6 134.3 %copy-start.13 = (bf16[384,1024]{0,1:T(8,128)(2,1)S(1)}, bf16[384,1024]{0,1:T(8,128)(2,1)}, u32[]{:S(2)}) copy-start(bf16[384,1024]{0,1:T(8,128)(2,1)} %copy-done.11) | copy-start | bytes 2359300
  1316.6 134.3 %copy-start.36 = (f32[1024]{0:T(1024)S(1)}, f32[1024]{0:T(1024)}, u32[]{:S(2)}) copy-start(f32[1024]{0:T(1024)} %copy-done.35) | copy-start | bytes 12292
  1316.6 134.3 %copy-start.38 = (f32[1024]{0:T(1024)S(1)}, f32[1024]{0:T(1024)}, u32[]{:S(2)}) copy-start(f32[1024]{0:T(1024)} %copy-done.37) | copy-start | bytes 12292
  1316.7 134.3 %copy-start.40 = (f32[384]{0:T(512)S(1)}, f32[384]{0:T(512)}, u32[]{:S(2)}) copy-start(f32[384]{0:T(512)} %param.18) | copy-start | bytes 4612
  (49 other events, 155.9 us)
Sparse Core Ops, SparseCore 0:
  17.3 30.2 all-gather.4
  54.8 110.6 reduce-scatter.8
  300.9 58.8 reduce-scatter.10
  361.8 28.4 all-gather.8
  392.3 28.4 all-gather.6
  423.0 144.5 reduce-scatter.16
  569.9 144.5 reduce-scatter.12
  801.8 58.8 reduce-scatter.18
  882.0 58.8 reduce-scatter.14
  945.2 28.4 all-gather.10
  978.7 43.3 reduce-scatter.20
  1216.4 96.6 all-reduce.8
  1316.3 74.2 all-reduce.10
  1393.0 57.8 reduce-scatter.22
